TPU v7x, 256 devices: a whole 4x4x8 slice. The times are simulated.
256 devices in a mesh: row: 16 (over z_hi, y), col: 16 (over z_lo, x, core).
Axes of the slice: x: 4, y: 4, z: 8 (z_hi: 4, z_lo: 2; z = z_hi * 2 + z_lo), core: 2. Of those that a mesh axis runs over, the one named last changes fastest.
Arguments:
- a11: float32 [256, 256], replicated, as said below
- linv11: float32 [256, 256], replicated, as said below
- a21: float32 [16384, 256], P(('row', 'col')), may hold values from -6 to 6
- l21: float32 [16384, 256], P(('row', 'col')), may hold values from -0.4 to 0.4
- a22: float32 [16384, 16384], P('row', 'col'), may hold values from -6 to 6
Outputs:
- diag_block: float32 [256, 256], replicated
- panel: float32 [16384, 256], P(('row', 'col'))
- trailing: float32 [16384, 16384], P('row', 'col')
Inputs may be any that keep to these rules, and one draw needn't show every extreme that they name: `a11`: symmetric. `linv11`: lower triangular with a positive diagonal.
All inputs are finite; a program needn't handle non-finite values.
Results may differ from a plain program's by a relative error of at most 0.00005.
Values sent between devices are 32-bit elements; how exact they have to be, the bound alone decides.
A program may use at most 64 MiB of HBM per device.

v0:
```python
import jax
import jax.numpy as jnp
from jax import lax
from jax.sharding import PartitionSpec as P


def spread(value, axis, source):
    kept = jnp.where(lax.axis_index(axis) == source, value, 0).astype(value.dtype)
    return lax.psum(kept, axis)


def mult(a, b):
    return jnp.dot(a, b, precision=lax.Precision.HIGHEST, preferred_element_type=jnp.float32)


def body(a11, linv11, a21, l21, a22):
    width = a21.shape[1]
    diag_block = mult(mult(linv11, a11), linv11.T)
    correction = 0.5 * mult(l21, diag_block)
    half = mult(a21, linv11.T) - correction
    panel = half - correction
    packed = jnp.concatenate([half, l21], axis=1)
    n_row = lax.axis_size("row")
    n_col = lax.axis_size("col")
    groups = n_row // n_col
    mine = lax.all_gather(packed, "col", axis=0, tiled=True)
    col_index = lax.axis_index("col")
    parts = spread(mine, "row", col_index * groups + 0)
    flipped = jnp.concatenate([parts[:, width:], parts[:, :width]], axis=1)
    trailing = a22 - mult(mine, flipped.T)
    return (diag_block, panel, trailing)


def solution(mesh):
    return jax.shard_map(
        body,
        mesh=mesh,
        in_specs=(P(), P(), P(("row", "col"), None), P(("row", "col"), None), P("row", "col")),
        out_specs=(P(), P(("row", "col"), None), P("row", "col")),
        check_vma=False,
    )
```

profile of v0, /device:TPU:4, one launch (start us, length us, event | category | flops | bytes accessed | tf_op | source)
XLA Modules:
  0.0 254.2 jit_solution(17430890461005125020)
XLA Ops:
  7.2 0.0 copy-start
  7.2 0.0 copy-start.3
  7.2 0.0 all-gather.2.cloned.1.call-start
  7.2 0.9 copy-done
  8.1 1.3 fusion.7
  9.5 0.4 fusion.8
  9.9 0.0 copy-start.2
  9.9 1.2 fusion.3
  11.1 1.8 fusion.6
  12.9 0.0 copy-done.3
  12.9 0.7 pad_maximum_fusion
  13.6 0.0 all-gather.2.cloned.1.call-update
  13.6 0.0 all-reduce.2.cloned.1.call-start
  13.7 38.5 %all-gather.2.cloned.1.call-done = f32[1024,512]{1,0:T(8,128)} async-done(((f32[64,512]{1,0:T(8,128)}), f32[1024,512]{1,0:T(8,128)}) %all-gather.2.cloned.1.call-update) | async-done | bytes 2097168 | tf_op jit(solution)/shard_map/all_gather | solution.py:26
  52.2 1.5 broadcast_select_fusion
  53.7 0.0 copy-done.2
  53.7 0.0 all-reduce.2.cloned.1.call-update
  53.7 0.0 copy-start.1
  53.7 182.1 %all-reduce.2.cloned.1.call-done = f32[1024,512]{1,0:T(8,128)} async-done(((f32[1024,512]{1,0:T(8,128)}), f32[1024,512]{1,0:T(8,128)}) %all-reduce.2.cloned.1.call-update) | async-done | bytes 2097168 | tf_op jit(solution)/shard_map/psum | solution.py:9
  235.8 1.7 fusion.5
  237.5 0.0 copy-done.1
  237.5 9.9 %convolution_subtract_fusion = f32[1024,1024]{1,0:T(8,128)} fusion(f32[1024,1024]{1,0:T(8,128)} %param.9, f32[1024,512]{1,0:T(8,128)S(1)} %copy-done.1, f32[1024,256]{1,0:T(8,128)S(1)} %get-tuple-element.4, f32[1024,256]{1,0:T(8,128)S(1)} %get-tuple-element.3), kind=kOutput, calls=%fused_computation | convolution fusion | flops 6444023808 | bytes 12582912 | tf_op jit(solution)/shard_map/dot_general | solution.py:13
Async XLA Ops:
  7.2 1.0 copy-start
  7.2 5.7 %copy-start.3 = (f32[64,256]{1,0:T(8,128)S(1)}, f32[64,256]{1,0:T(8,128)}, u32[]{:S(2)}) copy-start(f32[64,256]{1,0:T(8,128)} %param.8) | copy-start | bytes 196612
  7.2 45.0 %all-gather.2.cloned.1.call-start = ((), (), s32[]{:S(2)}) async-start(), calls=%async_computation | async-start | bytes 2228224 | tf_op jit(solution)/shard_map/all_gather | solution.py:26
  9.9 43.8 %copy-start.2 = (f32[256,256]{1,0:T(8,128)}, f32[256,256]{1,0:T(8,128)S(1)}, u32[]{:S(2)}) copy-start(f32[256,256]{1,0:T(8,128)S(1)} %fusion.8) | copy-start | bytes 786436
  13.6 222.2 %all-reduce.2.cloned.1.call-start = ((), (), s32[]{:S(2)}) async-start(), calls=%async_computation.1 | async-start | bytes 4194304 | tf_op jit(solution)/shard_map/psum | solution.py:9
  53.7 183.8 %copy-start.1 = (f32[1024,512]{1,0:T(8,128)S(1)}, f32[1024,512]{1,0:T(8,128)}, u32[]{:S(2)}) copy-start(f32[1024,512]{1,0:T(8,128)} %all-gather.2.cloned.1.call-done) | copy-start | bytes 6291460
Sparse Core Ops, SparseCore 0:
  13.7 38.3 all-gather.1
  55.4 180.3 all-reduce.1
where the time goes:
time: 255 us; the launch traced here: 254 us
  waiting for transfers between devices  221 us (87%)
  matrix products  14.6 us (6%)
  between operations  14.1 us (6%)
  local copies, waits for them, and re-layouts  2.58 us (1%)
    psum x1, waiting for transfers between devices, spread(): return lax.psum(kept, axis)  182 us
    all_gather x1, waiting for transfers between devices, body(): mine = lax.all_gather(packed, 'col', axis=0, tiled=True)  38.5 us
    dot_general x5, matrix products, mult(): jnp.dot(a, b, precision=lax.Precision.HIGHEST, preferred_element_type=jnp...  14.6 us
  transfers between devices with their start and end apart: 2, of which 2 were waited for; matrix products, arithmetic and copies ran while one was open for 0% of the time, Pallas kernels for 0%

commit v1 on v0

--- a/solution.py
+++ b/solution.py
@@ -6,7 +6,7 @@
 
 def spread(value, axis, source):
     kept = jnp.where(lax.axis_index(axis) == source, value, 0).astype(value.dtype)
-    return lax.psum(kept, axis)
+    return jnp.sum(lax.all_gather(kept, axis_name=axis), axis=0)
 
 
 def mult(a, b):

time: 255 us -> 461 us (1.81)
  waiting for transfers between devices: 221 us -> 414 us
  other arithmetic: 2.21 us -> 14.9 us
    all_gather x0 -> x1, waiting for transfers between devices: none -> 375 us  [spread(): return jnp.sum(lax.all_gather(kept, axis_name=axis), axis=0)]
    psum x1 -> x0, waiting for transfers between devices: 182 us -> none  [spread(): return lax.psum(kept, axis)]
    reduce_sum x0 -> x1, other arithmetic: none -> 12.7 us  [spread(): return jnp.sum(lax.all_gather(kept, axis_name=axis), axis=0)]
where the time goes in v1:
time: 461 us; the launch traced here: 460 us
  waiting for transfers between devices  414 us (90%)
  other arithmetic  14.9 us (3%)
  matrix products  14.6 us (3%)
  between operations  14.1 us (3%)
    all_gather x1, waiting for transfers between devices, spread(): return jnp.sum(lax.all_gather(kept, axis_name=axis), axis=0)  375 us
    all_gather x1, waiting for transfers between devices, body(): mine = lax.all_gather(packed, 'col', axis=0, tiled=True)  38.5 us
    dot_general x5, matrix products, mult(): jnp.dot(a, b, precision=lax.Precision.HIGHEST, preferred_element_type=jnp...  14.6 us
    reduce_sum x1, other arithmetic, spread(): return jnp.sum(lax.all_gather(kept, axis_name=axis), axis=0)  12.7 us
  transfers between devices with their start and end apart: 2, of which 2 were waited for; matrix products, arithmetic and copies ran while one was open for 0% of the time, Pallas kernels for 0%

profile of v1, /device:TPU:4, one launch (start us, length us, event | category | flops | bytes accessed | tf_op | source)
XLA Modules:
  0.0 460.2 jit_solution(10071502147895484908)
XLA Ops:
  7.2 0.0 copy-start
  7.2 0.0 copy-start.3
  7.2 0.0 all-gather.4.cloned.1.call-start
  7.2 0.9 copy-done
  8.1 1.3 fusion.7
  9.5 0.4 fusion.8
  9.9 0.0 copy-start.2
  9.9 1.2 fusion.3
  11.1 1.8 fusion.6
  12.9 0.0 copy-done.3
  12.9 0.7 pad_maximum_fusion
  13.6 0.0 all-gather.4.cloned.1.call-update
  13.6 0.0 all-gather.6.cloned.1.call-start
  13.7 38.5 %all-gather.4.cloned.1.call-done = f32[1024,512]{1,0:T(8,128)} async-done(((f32[64,512]{1,0:T(8,128)}), f32[1024,512]{1,0:T(8,128)}) %all-gather.4.cloned.1.call-update) | async-done | bytes 2097168 | tf_op jit(solution)/shard_map/all_gather | solution.py:26
  52.2 1.5 broadcast_select_fusion
  53.7 0.0 copy-done.2
  53.7 0.0 all-gather.6.cloned.1.call-update
  53.7 375.5 %all-gather.6.cloned.1.call-done = f32[16384,512]{1,0:T(8,128)} async-done(((f32[1024,512]{1,0:T(8,128)}), f32[16384,512]{1,0:T(8,128)}) %all-gather.6.cloned.1.call-update) | async-done | bytes 33554448 | tf_op jit(solution)/shard_map/all_gather | solution.py:9
  429.2 12.7 %reduce_sum.9 = f32[1024,512]{1,0:T(8,128)S(1)} reduce(f32[16,1024,512]{2,1,0:T(8,128)} %bitcast.12, f32[]{:T(128)} %constant.12.clone.1), dimensions={0}, to_apply=%region_0.1 | reduce | flops 7864320 | bytes 35651588 | tf_op jit(solution)/shard_map/reduce_sum | solution.py:9
  441.9 0.0 copy-start.1
  441.9 0.2 fusion.5
  442.1 1.4 copy-done.1
  443.5 9.8 %convolution_subtract_fusion = f32[1024,1024]{1,0:T(8,128)} fusion(f32[1024,1024]{1,0:T(8,128)} %param.9, f32[1024,512]{1,0:T(8,128)S(1)} %copy-done.1, f32[1024,256]{1,0:T(8,128)S(1)} %get-tuple-element.4, f32[1024,256]{1,0:T(8,128)S(1)} %get-tuple-element.3), kind=kOutput, calls=%fused_computation | convolution fusion | flops 6444023808 | bytes 12582912 | tf_op jit(solution)/shard_map/dot_general | solution.py:13
Async XLA Ops:
  7.2 1.0 copy-start
  7.2 5.7 %copy-start.3 = (f32[64,256]{1,0:T(8,128)S(1)}, f32[64,256]{1,0:T(8,128)}, u32[]{:S(2)}) copy-start(f32[64,256]{1,0:T(8,128)} %param.8) | copy-start | bytes 196612
  7.2 45.0 %all-gather.4.cloned.1.call-start = ((), (), s32[]{:S(2)}) async-start(), calls=%async_computation | async-start | bytes 2228224 | tf_op jit(solution)/shard_map/all_gather | solution.py:26
  9.9 43.8 %copy-start.2 = (f32[256,256]{1,0:T(8,128)}, f32[256,256]{1,0:T(8,128)S(1)}, u32[]{:S(2)}) copy-start(f32[256,256]{1,0:T(8,128)S(1)} %fusion.8) | copy-start | bytes 786436
  13.6 415.6 %all-gather.6.cloned.1.call-start = ((), (), s32[]{:S(2)}) async-start(), calls=%async_computation.1 | async-start | bytes 35651584 | tf_op jit(solution)/shard_map/all_gather | solution.py:9
  441.9 1.6 copy-start.1
Sparse Core Ops, SparseCore 0:
  13.7 38.3 all-gather.3
  55.2 373.9 all-gather.5
